TPU v7x, 32 devices: a whole 2x2x4 slice. The times are simulated.
32 devices in a mesh: depth: 2 (over x), map: 16 (over z, y, core).
Axes of the slice: x: 2, y: 2, z: 4, core: 2. Of those that a mesh axis runs over, the one named last changes fastest.
Arguments:
- velocity: float32 [3, 32, 512, 128], P(None, 'depth', 'map'), may hold values from -6 to 6
- stress: float32 [6, 32, 512, 128], P(None, 'depth', 'map'), may hold values from -6 to 6
- region: int32 [32, 512, 128], P('depth', 'map'), may hold values from 0 to 7
- lame_table: float32 [8], replicated, may hold values from 0.2 to 0.5
- shear_table: float32 [8], replicated, may hold values from 0.1 to 0.3
- buoyancy_table: float32 [8], replicated, may hold values from 0.6 to 1.2
- height: float32 [256, 4096], P('depth', 'map'), may hold values from -6 to 6
- discharge: float32 [2, 256, 4096], P(None, 'depth', 'map'), may hold values from -6 to 6
- face_depth: float32 [2, 256, 4096], P(None, 'depth', 'map'), may hold values from 0.5 to 2
- wet: int32 [256, 4096], P('depth', 'map'), may hold values 0 or 1
- seafloor_index: int32 [256, 4096], P('depth', 'map'), may hold values from 0 to 4095
Outputs:
- velocity_out: float32 [3, 32, 512, 128], P(None, 'depth', 'map')
- stress_out: float32 [6, 32, 512, 128], P(None, 'depth', 'map')
- height_out: float32 [256, 4096], P('depth', 'map')
- discharge_out: float32 [2, 256, 4096], P(None, 'depth', 'map')
Inputs may be any that keep to these rules, and one draw needn't show every extreme that they name: `wet`: 1 for a wet ocean cell, 0 for a dry one. `seafloor_index`: index k of the seafloor cell under an ocean cell, among the 32 x 128 crust cells of its own map column, counted row by row.
All inputs are finite; a program needn't handle non-finite values. No bound on the sum of `wet` on one device may be relied on, other than what follows from the above.
Results may differ from a plain program's by a relative error of at most 0.000054.
Values sent between devices are 32-bit elements; how exact they have to be, the bound alone decides.
No kernel may reach another device: no remote copies, remote signals or barrier semaphores. Data moves between devices by JAX's collectives and lax.ppermute only.
A program may use at most 64 MiB of HBM per device.

v0:
```python
import math

import jax
import jax.numpy as jnp
from jax import lax
from jax.sharding import PartitionSpec as P

ITERS = 3
OSTEPS = 2


near_coef = 9.0 / 8.0
far_coef = 1.0 / 24.0
time_step = 0.2
ocean_step = 0.2
gravity = 1.0


def extended(x, sides, width):
    for axis, dim in sides:
        peers, length = (lax.axis_size(axis), x.shape[dim])
        up = [(i, (i + 1) % peers) for i in range(peers - 1)]
        down = [(j, i) for i, j in up]
        last = lax.slice_in_dim(x, length - width, length, axis=dim)
        leading = lax.slice_in_dim(x, 0, width, axis=dim)
        before = lax.ppermute(last, axis, up)
        after = lax.ppermute(leading, axis, down)
        x = jnp.concatenate([before, x, after], axis=dim)
    return x


def broadcast(x, axis, root):
    mine = lax.axis_index(axis) == root
    return lax.psum(jnp.where(mine, x, jnp.zeros_like(x)), axis)


def passed_along(x, axis, by):
    peers = lax.axis_size(axis)
    pairs = [(i, i + by) for i in range(peers) if 0 <= i + by < peers]
    return lax.ppermute(x, axis, pairs)


def cells(padded, axis, offset, count):
    return lax.slice_in_dim(padded, offset, offset + count, axis=axis)


def forward_diff(padded, axis):
    count = padded.shape[axis] - 4
    return near_coef * (
        cells(padded, axis, 3, count) - cells(padded, axis, 2, count)
    ) - far_coef * (cells(padded, axis, 4, count) - cells(padded, axis, 1, count))


def backward_diff(padded, axis):
    count = padded.shape[axis] - 4
    return near_coef * (
        cells(padded, axis, 2, count) - cells(padded, axis, 1, count)
    ) - far_coef * (cells(padded, axis, 3, count) - cells(padded, axis, 0, count))


def forward_y(field):
    return near_coef * (jnp.roll(field, -1, 2) - field) - far_coef * (
        jnp.roll(field, -2, 2) - jnp.roll(field, 1, 2)
    )


def backward_y(field):
    return near_coef * (field - jnp.roll(field, 1, 2)) - far_coef * (
        jnp.roll(field, -1, 2) - jnp.roll(field, 2, 2)
    )


def lookup(region, table):
    total = jnp.zeros(region.shape, jnp.float32)
    for value in range(table.shape[0]):
        total = total + jnp.where(region == value, table[value], 0.0)
    return total


def seafloor_pick(tiles, seafloor_index):
    tile_rows = tiles.shape[1]
    tile_cols = tiles.shape[2]
    ocean_rows = seafloor_index.shape[0]
    ocean_cols = seafloor_index.shape[1]
    group = math.gcd(ocean_rows, 8)
    table = jnp.transpose(tiles, (1, 0, 2)).reshape(tile_rows, 2 * tile_cols)
    row_ids = lax.broadcasted_iota(jnp.int32, (1, 1, tile_rows), 2)
    col_ids = lax.broadcasted_iota(jnp.int32, (1, 1, tile_cols), 2)

    def one_block(indices):
        upper = indices // tile_cols
        lower = indices % tile_cols
        onehot = (upper[:, :, None] == row_ids).astype(jnp.float32)
        picked = jnp.einsum("rck,kn->rcn", onehot, table, precision=lax.Precision.HIGHEST)
        chosen = lower[:, :, None] == col_ids
        first = jnp.sum(jnp.where(chosen, picked[:, :, :tile_cols], 0.0), axis=2)
        second = jnp.sum(jnp.where(chosen, picked[:, :, tile_cols:], 0.0), axis=2)
        return jnp.stack([first, second])

    blocks = seafloor_index.reshape(ocean_rows // group, group, ocean_cols)
    result = lax.map(one_block, blocks)
    result = jnp.transpose(result, (1, 0, 2, 3)).reshape(2, ocean_rows, ocean_cols)
    return (result[0], result[1])


def per_device(
    velocity,
    stress,
    region,
    lame_table,
    shear_table,
    buoyancy_table,
    height,
    discharge,
    face_depth,
    wet,
    seafloor_index,
):
    lame = lookup(region, lame_table)
    shear = lookup(region, shear_table)
    buoyancy = lookup(region, buoyancy_table)
    speeds = velocity
    forces = stress
    lift = jnp.zeros((velocity.shape[2], velocity.shape[3]), jnp.float32)
    for turn in range(ITERS):
        map_part = extended(forces[0:3], (("map", 2),), 2)
        depth_part = extended(forces[2:5], (("depth", 1),), 2)
        speed_x = speeds[0] + time_step * buoyancy * (
            forward_diff(map_part[0], 1) + backward_y(forces[1]) + backward_diff(depth_part[0], 0)
        )
        speed_y = speeds[1] + time_step * buoyancy * (
            backward_diff(map_part[1], 1) + forward_y(forces[5]) + backward_diff(depth_part[1], 0)
        )
        speed_z = speeds[2] + time_step * buoyancy * (
            backward_diff(map_part[2], 1) + backward_y(forces[3]) + forward_diff(depth_part[2], 0)
        )
        speeds = jnp.stack([speed_x, speed_y, speed_z])
        lift = lift + time_step * speed_z[0]
        beside_all = extended(speeds, (("depth", 1), ("map", 2)), 2)
        speed_map = beside_all[:, 2:-2]
        speed_depth = beside_all[:, :, 2:-2]
        strain_x = backward_diff(speed_map[0], 1)
        strain_y = backward_y(speed_y)
        strain_z = backward_diff(speed_depth[2], 0)
        spread = strain_x + strain_y + strain_z
        forces = jnp.stack(
            [
                forces[0] + time_step * (lame * spread + 2.0 * shear * strain_x),
                forces[1]
                + time_step * shear * (forward_y(speed_x) + forward_diff(speed_map[1], 1)),
                forces[2]
                + time_step
                * shear
                * (forward_diff(speed_depth[0], 0) + forward_diff(speed_map[2], 1)),
                forces[3]
                + time_step * shear * (forward_diff(speed_depth[1], 0) + forward_y(speed_z)),
                forces[4] + time_step * (lame * spread + 2.0 * shear * strain_z),
                forces[5] + time_step * (lame * spread + 2.0 * shear * strain_y),
            ]
        )
    tiles = broadcast(jnp.stack([lift, speeds[2][0]]), "depth", 0)
    lift_at, rate_at = seafloor_pick(tiles, seafloor_index)
    wetness = wet.astype(jnp.float32)
    level = wetness * (height + lift_at)
    source = wetness * rate_at
    east_pair = passed_along(jnp.stack([level[:, :1], wetness[:, :1]]), "map", -1)
    north_pair = passed_along(jnp.stack([level[:1, :], wetness[:1, :]]), "depth", -1)
    wet_east = jnp.concatenate([wetness[:, 1:], east_pair[1]], axis=1)
    wet_north = jnp.concatenate([wetness[1:, :], north_pair[1]], axis=0)
    mask_x = wetness * wet_east
    mask_y = wetness * wet_north
    depth_x = face_depth[0] * mask_x
    depth_y = face_depth[1] * mask_y
    flux_x = discharge[0] * mask_x
    flux_y = discharge[1] * mask_y
    for turn in range(OSTEPS):
        if turn == 0:
            east_col = east_pair[0]
            north_row = north_pair[0]
        else:
            east_col = passed_along(level[:, :1], "map", -1)
            north_row = passed_along(level[:1, :], "depth", -1)
        level_east = jnp.concatenate([level[:, 1:], east_col], axis=1)
        level_north = jnp.concatenate([level[1:, :], north_row], axis=0)
        flux_x = flux_x - ocean_step * gravity * depth_x * (level_east - level)
        flux_y = flux_y - ocean_step * gravity * depth_y * (level_north - level)
        west_col = passed_along(flux_x[:, -1:], "map", 1)
        south_row = passed_along(flux_y[-1:, :], "depth", 1)
        flux_west = jnp.concatenate([west_col, flux_x[:, :-1]], axis=1)
        flux_south = jnp.concatenate([south_row, flux_y[:-1, :]], axis=0)
        level = (
            level
            - ocean_step * wetness * (flux_x - flux_west + (flux_y - flux_south))
            + ocean_step * source
        )
    return (speeds, forces, level, jnp.stack([flux_x, flux_y]))


def solution(mesh):
    return jax.shard_map(
        per_device,
        mesh=mesh,
        in_specs=(
            P(None, "depth", "map", None),
            P(None, "depth", "map", None),
            P("depth", "map", None),
            P(),
            P(),
            P(),
            P("depth", "map"),
            P(None, "depth", "map"),
            P(None, "depth", "map"),
            P("depth", "map"),
            P("depth", "map"),
        ),
        out_specs=(
            P(None, "depth", "map", None),
            P(None, "depth", "map", None),
            P("depth", "map"),
            P(None, "depth", "map"),
        ),
        check_vma=False,
    )
```

profile of v0, /device:TPU:7, one launch (start us, length us, event | category | flops | bytes accessed | tf_op | source)
XLA Modules:
  0.0 251.1 jit_solution(1492550919271240779)
XLA Ops:
  2.3 3.7 %collective-permute-start = (f32[3,16,2,128]{3,2,1,0:T(2,128)}, f32[3,16,2,128]{3,2,1,0:T(2,128)}, u32[]{:S(2)}, u32[]{:S(2)}) collective-permute-start(f32[3,16,2,128]{3,2,1,0:T(2,128)} %get-tuple-element.138), channel_id=1, source_target_pairs={{0,1},{1,2},{2,3},{3,4},{4,5},{5,6},{6,7},{7,8},{8,9},{9,10},{10,1... | collective-permute-start | bytes 147464 | tf_op jit(solution)/shard_map/ppermute | solution.py:26
  10.9 4.8 %collective-permute-start.3 = (f32[3,2,32,128]{3,2,1,0:T(8,128)}, f32[3,2,32,128]{3,2,1,0:T(8,128)}, u32[]{:S(2)}, u32[]{:S(2)}) collective-permute-start(f32[3,2,32,128]{3,2,1,0:T(8,128)} %get-tuple-element.143), channel_id=1, source_target_pairs={{16,0},{17,1},{18,2},{19,3},{20,4},{21,5},{22,6},{23,7},{24,8},{25... | collective-permute-start | bytes 294920 | tf_op jit(solution)/shard_map/ppermute | solution.py:27
  30.2 6.6 %fusion.30 = (f32[16,32,128]{2,1,0:T(8,128)S(1)}, f32[16,32,128]{2,1,0:T(8,128)S(1)}, pred[16,32,128]{2,1,0:T(8,128)(4,1)S(1)}, pred[16,32,128]{2,1,0:T(8,128)(4...) fusion(f32[3,16,32,128]{3,2,1,0:T(8,128)S(1)} %copy-done.1, ...), kind=kLoop, calls=%fused_computation.102 | loop fusion | flops 3211264 | bytes 4915232 | tf_op jit(solution)/shard_map/add | solution.py:128
  42.1 4.0 %collective-permute-start.5 = (f32[3,2,32,128]{3,2,1,0:T(8,128)S(1)}, f32[3,2,32,128]{3,2,1,0:T(8,128)S(1)}, u32[]{:S(2)}, u32[]{:S(2)}) collective-permute-start(f32[3,2,32,128]{3,2,1,0:T(8,128)S(1)} %get-tuple-element.190), channel_id=1, source_target_pairs={{16,0},{17,1},{18,2},{19,3},{20,4},{21,5},{22,6},{23,7},{24,8},{25... | collective-permute-start | bytes 294920 | tf_op jit(solution)/shard_map/ppermute | solution.py:27
  47.8 6.2 %collective-permute-start.6 = (f32[3,20,2,128]{3,2,1,0:T(2,128)S(1)}, f32[3,20,2,128]{3,2,1,0:T(2,128)S(1)}, u32[]{:S(2)}, u32[]{:S(2)}) collective-permute-start(f32[3,20,2,128]{3,2,1,0:T(2,128)S(1)} %get-tuple-element.160), channel_id=1, source_target_pairs={{0,1},{1,2},{2,3},{3,4},{4,5},{5,6},{6,7},{7,8},{8,9},{9,10},{10,1... | collective-permute-start | bytes 184328 | tf_op jit(solution)/shard_map/ppermute | solution.py:26
  56.2 4.2 %collective-permute-done.7 = f32[3,20,2,128]{3,2,1,0:T(2,128)S(1)} collective-permute-done((f32[3,20,2,128]{3,2,1,0:T(2,128)S(1)}, f32[3,20,2,128]{3,2,1,0:T(2,128)S(1)}, u32[]{:S(2)}, u32[]{:S(2)}) %collective-permute-start.7) | collective-permute-done | bytes 61472 | tf_op jit(solution)/shard_map/ppermute | solution.py:27
  60.5 10.9 %multiply_add_fusion.3 = (f32[16,32,128]{2,1,0:T(8,128)S(1)}, f32[16,32,128]{2,1,0:T(8,128)S(1)}, f32[16,32,128]{2,1,0:T(8,128)S(1)}, f32[16,32,128]{2,1,0:T(8,1...) fusion(f32[6,16,32,128]{3,2,1,0:T(8,128)S(1)} %copy-done, ...), kind=kLoop, calls=%fused_computation.482 | loop fusion | flops 3670016 | bytes 5505088 | tf_op jit(solution)/shard_map/add | solution.py:158
  75.4 2.4 collective-permute-start.9
  79.5 4.0 %collective-permute-start.11 = (f32[3,2,32,128]{3,2,1,0:T(8,128)S(1)}, f32[3,2,32,128]{3,2,1,0:T(8,128)S(1)}, u32[]{:S(2)}, u32[]{:S(2)}) collective-permute-start(f32[3,2,32,128]{3,2,1,0:T(8,128)S(1)} %get-tuple-element.185), channel_id=1, source_target_pairs={{16,0},{17,1},{18,2},{19,3},{20,4},{21,5},{22,6},{23,7},{24,8},{25... | collective-permute-start | bytes 294920 | tf_op jit(solution)/shard_map/ppermute | solution.py:27
  88.9 4.1 %collective-permute-start.13 = (f32[3,2,32,128]{3,2,1,0:T(8,128)S(1)}, f32[3,2,32,128]{3,2,1,0:T(8,128)S(1)}, u32[]{:S(2)}, u32[]{:S(2)}) collective-permute-start(f32[3,2,32,128]{3,2,1,0:T(8,128)S(1)} %get-tuple-element.180), channel_id=1, source_target_pairs={{16,0},{17,1},{18,2},{19,3},{20,4},{21,5},{22,6},{23,7},{24,8},{25... | collective-permute-start | bytes 294920 | tf_op jit(solution)/shard_map/ppermute | solution.py:27
  94.7 5.9 %collective-permute-start.14 = (f32[3,20,2,128]{3,2,1,0:T(2,128)S(1)}, f32[3,20,2,128]{3,2,1,0:T(2,128)S(1)}, u32[]{:S(2)}, u32[]{:S(2)}) collective-permute-start(f32[3,20,2,128]{3,2,1,0:T(2,128)S(1)} %get-tuple-element.155), channel_id=1, source_target_pairs={{0,1},{1,2},{2,3},{3,4},{4,5},{5,6},{6,7},{7,8},{8,9},{9,10},{10,1... | collective-permute-start | bytes 184328 | tf_op jit(solution)/shard_map/ppermute | solution.py:26
  104.0 3.1 %collective-permute-done.15 = f32[3,20,2,128]{3,2,1,0:T(2,128)S(1)} collective-permute-done((f32[3,20,2,128]{3,2,1,0:T(2,128)S(1)}, f32[3,20,2,128]{3,2,1,0:T(2,128)S(1)}, u32[]{:S(2)}, u32[]{:S(2)}) %collective-permute-start.15) | collective-permute-done | bytes 61472 | tf_op jit(solution)/shard_map/ppermute | solution.py:27
  113.9 2.4 collective-permute-start.17
  119.3 4.0 %collective-permute-start.19 = (f32[3,2,32,128]{3,2,1,0:T(8,128)S(1)}, f32[3,2,32,128]{3,2,1,0:T(8,128)S(1)}, u32[]{:S(2)}, u32[]{:S(2)}) collective-permute-start(f32[3,2,32,128]{3,2,1,0:T(8,128)S(1)} %get-tuple-element.175), channel_id=1, source_target_pairs={{16,0},{17,1},{18,2},{19,3},{20,4},{21,5},{22,6},{23,7},{24,8},{25... | collective-permute-start | bytes 294920 | tf_op jit(solution)/shard_map/ppermute | solution.py:27
  126.7 7.3 %psum.7 = f32[32,256]{1,0:T(8,128)S(1)} all-reduce(f32[32,256]{1,0:T(8,128)S(1)} %copy_bitcast_fusion), channel_id=1, replica_groups=mesh['depth'=2,'map'=16] {'depth'}, use_global_device_ids=true, to_apply=%region_0.1 | all-reduce | flops 8192 | bytes 65536 | tf_op jit(solution)/shard_map/psum | solution.py:34
  134.0 52.3 %while.13 = (s32[]{:T(128)}, f32[16,2,8,256]{3,2,1,0:T(8,128)}, s32[16,8,256]{2,1,0:T(8,128)}, f32[32,256]{1,0:T(8,128)S(1)}, s32[]{:T(128)}) while((s32[]{:T(128)}, f32[16,2,8,256]{3,2,1,0:T(8,128)}, s32[16,8,256]{2,1,0:T(8,128)}, f32[32,256]{1,0:T(8,128)S(1)}, s32[]{:T(128)}) %tuple.162), condition=%wide.region_4.5_spmd.clone, body=%wide.region_1.4_spmd.clone.sunk | while | flops 202754048 | bytes 4330053 | solution.py:101
  187.4 2.4 fusion.105
  196.6 5.0 %collective-permute-start.24 = (f32[2,128,1]{1,2,0:T(1,128)S(1)}, f32[2,128,1]{1,2,0:T(1,128)S(1)}, u32[]{:S(2)}, u32[]{:S(2)}) collective-permute-start(f32[2,128,1]{1,2,0:T(1,128)S(1)} %pad_maximum_fusion.64), channel_id=1, source_target_pairs={{1,0},{2,1},{3,2},{4,3},{5,4},{6,5},{7,6},{8,7},{9,8},{10,9},{11,1... | collective-permute-start | bytes 3080 | tf_op jit(solution)/shard_map/ppermute | solution.py:40
  206.8 4.6 %collective-permute-start.25 = (f32[128,1]{1,0:T(8,128)S(1)}, f32[128,1]{1,0:T(8,128)S(1)}, u32[]{:S(2)}, u32[]{:S(2)}) collective-permute-start(f32[128,1]{1,0:T(8,128)S(1)} %slice.2012), channel_id=1, source_target_pairs={{0,1},{1,2},{2,3},{3,4},{4,5},{5,6},{6,7},{7,8},{8,9},{9,10},{10,1... | collective-permute-start | bytes 1544 | tf_op jit(solution)/shard_map/ppermute | solution.py:40
  212.8 2.9 %collective-permute-done.27 = f32[1,256]{1,0:T(1,128)S(1)} collective-permute-done((f32[1,256]{1,0:T(1,128)S(1)}, f32[1,256]{1,0:T(1,128)S(1)}, u32[]{:S(2)}, u32[]{:S(2)}) %collective-permute-start.27) | collective-permute-done | bytes 1056 | tf_op jit(solution)/shard_map/ppermute | solution.py:40
  221.4 4.0 %collective-permute-start.21 = (f32[3,2,32,128]{3,2,1,0:T(8,128)S(1)}, f32[3,2,32,128]{3,2,1,0:T(8,128)S(1)}, u32[]{:S(2)}, u32[]{:S(2)}) collective-permute-start(f32[3,2,32,128]{3,2,1,0:T(8,128)S(1)} %get-tuple-element.170), channel_id=1, source_target_pairs={{16,0},{17,1},{18,2},{19,3},{20,4},{21,5},{22,6},{23,7},{24,8},{25... | collective-permute-start | bytes 294920 | tf_op jit(solution)/shard_map/ppermute | solution.py:27
  225.8 5.4 %collective-permute-start.29 = (f32[128,1]{1,0:T(8,128)S(1)}, f32[128,1]{1,0:T(8,128)S(1)}, u32[]{:S(2)}, u32[]{:S(2)}) collective-permute-start(f32[128,1]{1,0:T(8,128)S(1)} %slice.2025), channel_id=1, source_target_pairs={{0,1},{1,2},{2,3},{3,4},{4,5},{5,6},{6,7},{7,8},{8,9},{9,10},{10,1... | collective-permute-start | bytes 1544 | tf_op jit(solution)/shard_map/ppermute | solution.py:40
  236.3 3.1 %collective-permute-start.22 = (f32[3,20,2,128]{3,2,1,0:T(2,128)S(1)}, f32[3,20,2,128]{3,2,1,0:T(2,128)S(1)}, u32[]{:S(2)}, u32[]{:S(2)}) collective-permute-start(f32[3,20,2,128]{3,2,1,0:T(2,128)S(1)} %get-tuple-element.150), channel_id=1, source_target_pairs={{0,1},{1,2},{2,3},{3,4},{4,5},{5,6},{6,7},{7,8},{8,9},{9,10},{10,1... | collective-permute-start | bytes 184328 | tf_op jit(solution)/shard_map/ppermute | solution.py:26
  241.8 4.2 %collective-permute-done.23 = f32[3,20,2,128]{3,2,1,0:T(2,128)S(1)} collective-permute-done((f32[3,20,2,128]{3,2,1,0:T(2,128)S(1)}, f32[3,20,2,128]{3,2,1,0:T(2,128)S(1)}, u32[]{:S(2)}, u32[]{:S(2)}) %collective-permute-start.23) | collective-permute-done | bytes 61472 | tf_op jit(solution)/shard_map/ppermute | solution.py:27
  (392 shorter events, 143.1 us)
Async XLA Ops:
  2.3 25.8 %collective-permute-start = (f32[3,16,2,128]{3,2,1,0:T(2,128)}, f32[3,16,2,128]{3,2,1,0:T(2,128)}, u32[]{:S(2)}, u32[]{:S(2)}) collective-permute-start(f32[3,16,2,128]{3,2,1,0:T(2,128)} %get-tuple-element.138), channel_id=1, source_target_pairs={{0,1},{1,2},{2,3},{3,4},{4,5},{5,6},{6,7},{7,8},{8,9},{9,10},{10,1... | collective-permute-start | bytes 147464 | tf_op jit(solution)/shard_map/ppermute | solution.py:26
  6.0 22.1 %collective-permute-start.1 = (f32[3,16,2,128]{3,2,1,0:T(2,128)}, f32[3,16,2,128]{3,2,1,0:T(2,128)}, u32[]{:S(2)}, u32[]{:S(2)}) collective-permute-start(f32[3,16,2,128]{3,2,1,0:T(2,128)} %get-tuple-element.139), channel_id=1, source_target_pairs={{1,0},{2,1},{3,2},{4,3},{5,4},{6,5},{7,6},{8,7},{9,8},{10,9},{11,1... | collective-permute-start | bytes 147464 | tf_op jit(solution)/shard_map/ppermute | solution.py:27
  9.6 19.8 %collective-permute-start.2 = (f32[3,2,32,128]{3,2,1,0:T(8,128)}, f32[3,2,32,128]{3,2,1,0:T(8,128)S(1)}, u32[]{:S(2)}, u32[]{:S(2)}) collective-permute-start(f32[3,2,32,128]{3,2,1,0:T(8,128)} %get-tuple-element.142), channel_id=1, source_target_pairs={{0,16},{1,17},{2,18},{3,19},{4,20},{5,21},{6,22},{7,23},{8,24},{9,... | collective-permute-start | bytes 294920 | tf_op jit(solution)/shard_map/ppermute | solution.py:26
  10.9 18.5 %collective-permute-start.3 = (f32[3,2,32,128]{3,2,1,0:T(8,128)}, f32[3,2,32,128]{3,2,1,0:T(8,128)}, u32[]{:S(2)}, u32[]{:S(2)}) collective-permute-start(f32[3,2,32,128]{3,2,1,0:T(8,128)} %get-tuple-element.143), channel_id=1, source_target_pairs={{16,0},{17,1},{18,2},{19,3},{20,4},{21,5},{22,6},{23,7},{24,8},{25... | collective-permute-start | bytes 294920 | tf_op jit(solution)/shard_map/ppermute | solution.py:27
  47.8 8.4 %collective-permute-start.6 = (f32[3,20,2,128]{3,2,1,0:T(2,128)S(1)}, f32[3,20,2,128]{3,2,1,0:T(2,128)S(1)}, u32[]{:S(2)}, u32[]{:S(2)}) collective-permute-start(f32[3,20,2,128]{3,2,1,0:T(2,128)S(1)} %get-tuple-element.160), channel_id=1, source_target_pairs={{0,1},{1,2},{2,3},{3,4},{4,5},{5,6},{6,7},{7,8},{8,9},{9,10},{10,1... | collective-permute-start | bytes 184328 | tf_op jit(solution)/shard_map/ppermute | solution.py:26
  54.0 6.4 %collective-permute-start.7 = (f32[3,20,2,128]{3,2,1,0:T(2,128)S(1)}, f32[3,20,2,128]{3,2,1,0:T(2,128)S(1)}, u32[]{:S(2)}, u32[]{:S(2)}) collective-permute-start(f32[3,20,2,128]{3,2,1,0:T(2,128)S(1)} %get-tuple-element.161), channel_id=1, source_target_pairs={{1,0},{2,1},{3,2},{4,3},{5,4},{6,5},{7,6},{8,7},{9,8},{10,9},{11,1... | collective-permute-start | bytes 184328 | tf_op jit(solution)/shard_map/ppermute | solution.py:27
  73.5 10.1 %collective-permute-start.8 = (f32[3,16,2,128]{3,2,1,0:T(2,128)S(1)}, f32[3,16,2,128]{3,2,1,0:T(2,128)S(1)}, u32[]{:S(2)}, u32[]{:S(2)}) collective-permute-start(f32[3,16,2,128]{3,2,1,0:T(2,128)S(1)} %get-tuple-element.181), channel_id=1, source_target_pairs={{0,1},{1,2},{2,3},{3,4},{4,5},{5,6},{6,7},{7,8},{8,9},{9,10},{10,1... | collective-permute-start | bytes 147464 | tf_op jit(solution)/shard_map/ppermute | solution.py:26
  75.4 8.2 %collective-permute-start.9 = (f32[3,16,2,128]{3,2,1,0:T(2,128)S(1)}, f32[3,16,2,128]{3,2,1,0:T(2,128)S(1)}, u32[]{:S(2)}, u32[]{:S(2)}) collective-permute-start(f32[3,16,2,128]{3,2,1,0:T(2,128)S(1)} %get-tuple-element.182), channel_id=1, source_target_pairs={{1,0},{2,1},{3,2},{4,3},{5,4},{6,5},{7,6},{8,7},{9,8},{10,9},{11,1... | collective-permute-start | bytes 147464 | tf_op jit(solution)/shard_map/ppermute | solution.py:27
  78.2 6.3 %collective-permute-start.10 = (f32[3,2,32,128]{3,2,1,0:T(8,128)S(1)}, f32[3,2,32,128]{3,2,1,0:T(8,128)S(1)}, u32[]{:S(2)}, u32[]{:S(2)}) collective-permute-start(f32[3,2,32,128]{3,2,1,0:T(8,128)S(1)} %get-tuple-element.186), channel_id=1, source_target_pairs={{0,16},{1,17},{2,18},{3,19},{4,20},{5,21},{6,22},{7,23},{8,24},{9,... | collective-permute-start | bytes 294920 | tf_op jit(solution)/shard_map/ppermute | solution.py:26
  79.5 5.9 %collective-permute-start.11 = (f32[3,2,32,128]{3,2,1,0:T(8,128)S(1)}, f32[3,2,32,128]{3,2,1,0:T(8,128)S(1)}, u32[]{:S(2)}, u32[]{:S(2)}) collective-permute-start(f32[3,2,32,128]{3,2,1,0:T(8,128)S(1)} %get-tuple-element.185), channel_id=1, source_target_pairs={{16,0},{17,1},{18,2},{19,3},{20,4},{21,5},{22,6},{23,7},{24,8},{25... | collective-permute-start | bytes 294920 | tf_op jit(solution)/shard_map/ppermute | solution.py:27
  87.6 6.0 %collective-permute-start.12 = (f32[3,2,32,128]{3,2,1,0:T(8,128)S(1)}, f32[3,2,32,128]{3,2,1,0:T(8,128)S(1)}, u32[]{:S(2)}, u32[]{:S(2)}) collective-permute-start(f32[3,2,32,128]{3,2,1,0:T(8,128)S(1)} %get-tuple-element.179), channel_id=1, source_target_pairs={{0,16},{1,17},{2,18},{3,19},{4,20},{5,21},{6,22},{7,23},{8,24},{9,... | collective-permute-start | bytes 294920 | tf_op jit(solution)/shard_map/ppermute | solution.py:26
  94.7 9.3 %collective-permute-start.14 = (f32[3,20,2,128]{3,2,1,0:T(2,128)S(1)}, f32[3,20,2,128]{3,2,1,0:T(2,128)S(1)}, u32[]{:S(2)}, u32[]{:S(2)}) collective-permute-start(f32[3,20,2,128]{3,2,1,0:T(2,128)S(1)} %get-tuple-element.155), channel_id=1, source_target_pairs={{0,1},{1,2},{2,3},{3,4},{4,5},{5,6},{6,7},{7,8},{8,9},{9,10},{10,1... | collective-permute-start | bytes 184328 | tf_op jit(solution)/shard_map/ppermute | solution.py:26
  100.6 6.4 %collective-permute-start.15 = (f32[3,20,2,128]{3,2,1,0:T(2,128)S(1)}, f32[3,20,2,128]{3,2,1,0:T(2,128)S(1)}, u32[]{:S(2)}, u32[]{:S(2)}) collective-permute-start(f32[3,20,2,128]{3,2,1,0:T(2,128)S(1)} %get-tuple-element.156), channel_id=1, source_target_pairs={{1,0},{2,1},{3,2},{4,3},{5,4},{6,5},{7,6},{8,7},{9,8},{10,9},{11,1... | collective-permute-start | bytes 184328 | tf_op jit(solution)/shard_map/ppermute | solution.py:27
  112.0 11.4 %collective-permute-start.16 = (f32[3,16,2,128]{3,2,1,0:T(2,128)S(1)}, f32[3,16,2,128]{3,2,1,0:T(2,128)S(1)}, u32[]{:S(2)}, u32[]{:S(2)}) collective-permute-start(f32[3,16,2,128]{3,2,1,0:T(2,128)S(1)} %get-tuple-element.171), channel_id=1, source_target_pairs={{0,1},{1,2},{2,3},{3,4},{4,5},{5,6},{6,7},{7,8},{8,9},{9,10},{10,1... | collective-permute-start | bytes 147464 | tf_op jit(solution)/shard_map/ppermute | solution.py:26
  113.9 9.5 %collective-permute-start.17 = (f32[3,16,2,128]{3,2,1,0:T(2,128)S(1)}, f32[3,16,2,128]{3,2,1,0:T(2,128)S(1)}, u32[]{:S(2)}, u32[]{:S(2)}) collective-permute-start(f32[3,16,2,128]{3,2,1,0:T(2,128)S(1)} %get-tuple-element.172), channel_id=1, source_target_pairs={{1,0},{2,1},{3,2},{4,3},{5,4},{6,5},{7,6},{8,7},{9,8},{10,9},{11,1... | collective-permute-start | bytes 147464 | tf_op jit(solution)/shard_map/ppermute | solution.py:27
  118.1 6.4 %collective-permute-start.18 = (f32[3,2,32,128]{3,2,1,0:T(8,128)S(1)}, f32[3,2,32,128]{3,2,1,0:T(8,128)S(1)}, u32[]{:S(2)}, u32[]{:S(2)}) collective-permute-start(f32[3,2,32,128]{3,2,1,0:T(8,128)S(1)} %get-tuple-element.176), channel_id=1, source_target_pairs={{0,16},{1,17},{2,18},{3,19},{4,20},{5,21},{6,22},{7,23},{8,24},{9,... | collective-permute-start | bytes 294920 | tf_op jit(solution)/shard_map/ppermute | solution.py:26
  196.6 8.2 %collective-permute-start.24 = (f32[2,128,1]{1,2,0:T(1,128)S(1)}, f32[2,128,1]{1,2,0:T(1,128)S(1)}, u32[]{:S(2)}, u32[]{:S(2)}) collective-permute-start(f32[2,128,1]{1,2,0:T(1,128)S(1)} %pad_maximum_fusion.64), channel_id=1, source_target_pairs={{1,0},{2,1},{3,2},{4,3},{5,4},{6,5},{7,6},{8,7},{9,8},{10,9},{11,1... | collective-permute-start | bytes 3080 | tf_op jit(solution)/shard_map/ppermute | solution.py:40
  206.8 6.0 %collective-permute-start.25 = (f32[128,1]{1,0:T(8,128)S(1)}, f32[128,1]{1,0:T(8,128)S(1)}, u32[]{:S(2)}, u32[]{:S(2)}) collective-permute-start(f32[128,1]{1,0:T(8,128)S(1)} %slice.2012), channel_id=1, source_target_pairs={{0,1},{1,2},{2,3},{3,4},{4,5},{5,6},{6,7},{7,8},{8,9},{9,10},{10,1... | collective-permute-start | bytes 1544 | tf_op jit(solution)/shard_map/ppermute | solution.py:40
  215.9 9.6 %collective-permute-start.28 = (f32[128,1]{1,0:T(8,128)S(1)}, f32[128,1]{1,0:T(8,128)S(1)}, u32[]{:S(2)}, u32[]{:S(2)}) collective-permute-start(f32[128,1]{1,0:T(8,128)S(1)} %slice.2024), channel_id=1, source_target_pairs={{1,0},{2,1},{3,2},{4,3},{5,4},{6,5},{7,6},{8,7},{9,8},{10,9},{11,1... | collective-permute-start | bytes 1544 | tf_op jit(solution)/shard_map/ppermute | solution.py:40
  218.0 7.6 %collective-permute-start.30 = (f32[1,256]{1,0:T(1,128)S(1)}, f32[1,256]{1,0:T(1,128)S(1)}, u32[]{:S(2)}, u32[]{:S(2)}) collective-permute-start(f32[1,256]{1,0:T(1,128)S(1)} %slice.2028), channel_id=1, source_target_pairs={{16,0},{17,1},{18,2},{19,3},{20,4},{21,5},{22,6},{23,7},{24,8},{25... | collective-permute-start | bytes 3080 | tf_op jit(solution)/shard_map/ppermute | solution.py:40
  220.1 16.2 %collective-permute-start.20 = (f32[3,2,32,128]{3,2,1,0:T(8,128)S(1)}, f32[3,2,32,128]{3,2,1,0:T(8,128)S(1)}, u32[]{:S(2)}, u32[]{:S(2)}) collective-permute-start(f32[3,2,32,128]{3,2,1,0:T(8,128)S(1)} %get-tuple-element.169), channel_id=1, source_target_pairs={{0,16},{1,17},{2,18},{3,19},{4,20},{5,21},{6,22},{7,23},{8,24},{9,... | collective-permute-start | bytes 294920 | tf_op jit(solution)/shard_map/ppermute | solution.py:26
  221.4 14.9 %collective-permute-start.21 = (f32[3,2,32,128]{3,2,1,0:T(8,128)S(1)}, f32[3,2,32,128]{3,2,1,0:T(8,128)S(1)}, u32[]{:S(2)}, u32[]{:S(2)}) collective-permute-start(f32[3,2,32,128]{3,2,1,0:T(8,128)S(1)} %get-tuple-element.170), channel_id=1, source_target_pairs={{16,0},{17,1},{18,2},{19,3},{20,4},{21,5},{22,6},{23,7},{24,8},{25... | collective-permute-start | bytes 294920 | tf_op jit(solution)/shard_map/ppermute | solution.py:27
  225.8 7.4 %collective-permute-start.29 = (f32[128,1]{1,0:T(8,128)S(1)}, f32[128,1]{1,0:T(8,128)S(1)}, u32[]{:S(2)}, u32[]{:S(2)}) collective-permute-start(f32[128,1]{1,0:T(8,128)S(1)} %slice.2025), channel_id=1, source_target_pairs={{0,1},{1,2},{2,3},{3,4},{4,5},{5,6},{6,7},{7,8},{8,9},{9,10},{10,1... | collective-permute-start | bytes 1544 | tf_op jit(solution)/shard_map/ppermute | solution.py:40
  239.5 6.6 %collective-permute-start.23 = (f32[3,20,2,128]{3,2,1,0:T(2,128)S(1)}, f32[3,20,2,128]{3,2,1,0:T(2,128)S(1)}, u32[]{:S(2)}, u32[]{:S(2)}) collective-permute-start(f32[3,20,2,128]{3,2,1,0:T(2,128)S(1)} %get-tuple-element.151), channel_id=1, source_target_pairs={{1,0},{2,1},{3,2},{4,3},{5,4},{6,5},{7,6},{8,7},{9,8},{10,9},{11,1... | collective-permute-start | bytes 184328 | tf_op jit(solution)/shard_map/ppermute | solution.py:27
  (72 other events, 379.0 us)
where the time goes:
time: 254 us; the launch traced here: 251 us
  starting transfers between devices  91.2 us (36%)
  other arithmetic  72.3 us (28%)
  local copies, waits for them, and re-layouts  39.5 us (16%)
  waiting for transfers between devices  21.9 us (9%)
  matrix products  16.4 us (6%)
  blocking collectives  7.31 us (3%)
    ppermute x12, starting transfers between devices, extended(): after = lax.ppermute(leading, axis, down)  37.7 us
    ppermute x12, starting transfers between devices, extended(): before = lax.ppermute(last, axis, up)  30.5 us
    ppermute x8, starting transfers between devices, passed_along(): return lax.ppermute(x, axis, pairs)  23 us
    dot_general x16, matrix products, one_block(): jnp.einsum('rck,kn->rcn', onehot, table, precision=lax.Precision.HIGHEST)  16.4 us
    ppermute x12, waiting for transfers between devices, extended(): after = lax.ppermute(leading, axis, down)  15.4 us
    select_n x16, other arithmetic, one_block(): lower = indices % tile_cols  11.3 us
    select_n x16, other arithmetic, one_block(): upper = indices // tile_cols  11.3 us
    add x2, other arithmetic, per_device(): forces[5] + time_step * (lame * spread + 2.0 * shear * strain_y)  11.2 us
  transfers between devices with their start and end apart: 32, of which 11 were waited for; matrix products, arithmetic and copies ran while one was open for 10% of the time, Pallas kernels for 0%

commit v1 on v0

v1 whole, which is shorter than its diff:
```python
import functools

import jax
import jax.numpy as jnp
from jax import lax
from jax.experimental import pallas as pl
from jax.experimental.pallas import tpu as pltpu
from jax.sharding import PartitionSpec as P

ITERS = 3
OSTEPS = 2
LANES = 128
PAD = 8

near_coef = 9.0 / 8.0
far_coef = 1.0 / 24.0
time_step = 0.2
ocean_step = 0.2
gravity = 1.0

VMEM = pl.BlockSpec(memory_space=pltpu.VMEM)
SMEM = pl.BlockSpec(memory_space=pltpu.SMEM)
ANY = pl.BlockSpec(memory_space=pl.ANY)
F32 = jnp.float32

BACK = (2, 1)
FORTH = (1, 2)
STRESS_MAP = ((0, FORTH), (1, BACK), (2, BACK))
STRESS_DEPTH = ((2, BACK), (3, BACK), (4, FORTH))
SPEED_MAP = ((0, BACK), (1, FORTH), (2, FORTH))
SPEED_DEPTH = ((0, FORTH), (1, FORTH), (2, BACK))
SLOTS = 5


def slots(spec, side):
    found = {}
    for field, need in spec:
        cells = range(-need[0], 0) if side == 0 else range(need[1])
        for cell in cells:
            found[(field, cell)] = len(found)
    return found


def swap_pairs(count):
    first = [(i, i ^ 1) for i in range(count) if i ^ 1 < count]
    second = [(i, i + 1) for i in range(1, count - 1, 2)]
    return first, sorted(second + [(j, i) for i, j in second])


def swap(x, axis, phase):
    return lax.ppermute(x, axis, swap_pairs(lax.axis_size(axis))[phase])


def even(axis):
    return lax.rem(lax.axis_index(axis), 2) == 0


def roll(x, by):
    return pltpu.roll(x, by % x.shape[1], 1)


def diff_forward(at):
    return near_coef * (at(1) - at(0)) - far_coef * (at(2) - at(-1))


def diff_backward(at):
    return near_coef * (at(0) - at(-1)) - far_coef * (at(1) - at(-2))


def forward_y(x):
    return near_coef * (roll(x, -1) - x) - far_coef * (roll(x, -2) - roll(x, 1))


def backward_y(x):
    return near_coef * (x - roll(x, 1)) - far_coef * (roll(x, -1) - roll(x, 2))


def emit(spec, cell, size, parity_even, outs, store):
    def fill(out, side):
        for (field, offset), slot in slots(spec, side).items():
            store(out, slot, cell(field, size + offset if side == 0 else offset))

    @pl.when(parity_even)
    def _():
        fill(outs[0], 0)
        if len(outs) > 1:
            fill(outs[1], 1)

    @pl.when(jnp.logical_not(parity_even))
    def _():
        fill(outs[0], 1)
        if len(outs) > 1:
            fill(outs[1], 0)


def store_slot(out, slot, value):
    out[slot] = value


def emit_all(map_spec, depth_spec, read, layers, columns, depth_outs, map_outs):
    emit(depth_spec, lambda f, i: read(f, i, None), layers, even("depth"), depth_outs, store_slot)
    emit(map_spec, lambda f, i: read(f, None, i), columns, even("map"), map_outs, store_slot)


def edge_kernel(n_depth, ocean_n, layers, columns, stress, *refs):
    ocean = refs[:ocean_n]
    refs = refs[ocean_n:]
    depth_outs, map_outs = refs[:n_depth], refs[n_depth : n_depth + 2]
    low_c, high_c, low_d, high_d, low_o, high_o, sem = refs[n_depth + 2 :]
    copies = [
        (stress.at[pl.ds(0, 3), :, pl.ds(0, PAD)], low_c),
        (stress.at[pl.ds(0, 3), :, pl.ds(columns - PAD, PAD)], high_c),
        (stress.at[pl.ds(2, 3), pl.ds(0, 2)], low_d),
        (stress.at[pl.ds(2, 3), pl.ds(layers - 2, 2)], high_d),
    ]
    rows = ocean[0].shape[-2]
    for i, ref in enumerate(ocean):
        copies.append((ref.at[pl.ds(0, PAD)], low_o.at[i]))
        copies.append((ref.at[pl.ds(rows - PAD, PAD)], high_o.at[i]))
    copies = [pltpu.make_async_copy(a, b, sem.at[i]) for i, (a, b) in enumerate(copies)]
    for copy in copies:
        copy.start()
    for copy in copies:
        copy.wait()

    def read(field, layer, column):
        if column is None:
            return low_d[field - 2, layer] if layer < 2 else high_d[field - 2, layer - (layers - 2)]
        if column < PAD:
            return low_c[field, :, column]
        return high_c[field, :, column - (columns - PAD)]

    emit_all(STRESS_MAP, STRESS_DEPTH, read, layers, columns, depth_outs, map_outs)
    tiles = low_o.shape[2] // LANES

    def rows_out(out, side):
        source, first = (high_o, PAD - 2) if side == 0 else (low_o, 0)
        for i in range(ocean_n):
            for k in range(2):
                for t in range(tiles):
                    line = (i * 2 + k) * tiles + t
                    part = source[i, pl.ds(first + k, 1), pl.ds(t * LANES, LANES)]
                    out[SLOTS, pl.ds(line, 1), :] = part

    @pl.when(even("depth"))
    def _():
        rows_out(depth_outs[0], 0)
        if n_depth > 1:
            rows_out(depth_outs[1], 1)

    @pl.when(jnp.logical_not(even("depth")))
    def _():
        rows_out(depth_outs[0], 1)
        if n_depth > 1:
            rows_out(depth_outs[1], 0)


def material_kernel(lame_t, shear_t, buoy_t, region, dtb, dtl, dts):
    def body(p, _):
        r = region[p]
        b = jnp.full(r.shape, time_step * buoy_t[0], F32)
        l = jnp.full(r.shape, time_step * lame_t[0], F32)
        s = jnp.full(r.shape, time_step * shear_t[0], F32)
        for value in range(1, buoy_t.shape[0]):
            here = r == value
            b = jnp.where(here, time_step * buoy_t[value], b)
            l = jnp.where(here, time_step * lame_t[value], l)
            s = jnp.where(here, time_step * shear_t[value], s)
        dtb[p] = b
        dtl[p] = l
        dts[p] = s
        return 0

    lax.fori_loop(0, region.shape[0], body, 0)


def take_halos(spec, axis, received, below, above):
    zero = jnp.zeros(below.shape, F32)

    def halo(i):
        return received[i][0:SLOTS] if i < len(received) else zero

    @pl.when(even(axis))
    def _():
        above[...] = halo(0)
        below[...] = halo(1)

    @pl.when(jnp.logical_not(even(axis)))
    def _():
        below[...] = halo(0)
        above[...] = halo(1)


def build_map(spec, source, wide, received, layers, columns):
    def body(p, _):
        for field, _need in spec:
            wide[field, p, pl.ds(PAD, columns)] = source[field, p]
        return 0

    lax.fori_loop(0, layers, body, 0, unroll=4)

    def put(ref, side):
        for (field, offset), slot in slots(spec, side).items():
            at = PAD + offset if side == 0 else PAD + columns + offset
            wide[field, :, at] = ref[slot]

    @pl.when(even("map"))
    def _():
        put(received[0], 1)
        put(received[1], 0)

    @pl.when(jnp.logical_not(even("map")))
    def _():
        put(received[0], 0)
        put(received[1], 1)


def half_step(kind, n_depth, last, refs):
    layers, columns = refs[0].shape[1:3]
    if kind == "speed":
        speed, stress, dtb, lift_in = refs[:4]
        moving, n = stress, 4
        map_spec, depth_spec, out_map, out_depth = STRESS_MAP, STRESS_DEPTH, SPEED_MAP, SPEED_DEPTH
    else:
        stress, speed, dtl, dts = refs[:4]
        moving, n = speed, 4
        map_spec, depth_spec, out_map, out_depth = SPEED_MAP, SPEED_DEPTH, STRESS_MAP, STRESS_DEPTH
    recv_depth, recv_map = refs[n : n + n_depth], refs[n + n_depth : n + n_depth + 2]
    outs = refs[n + n_depth + 2 :]
    below, above, wide = outs[-3:]
    new = outs[0]
    outs = outs[1:-3]
    if kind == "speed":
        lift_out, outs = outs[0], outs[1:]
    take_halos(depth_spec, "depth", recv_depth, below, above)
    build_map(map_spec, moving, wide, recv_map, layers, columns)
    low, high = slots(depth_spec, 0), slots(depth_spec, 1)

    def layer(p):
        def z(field):
            def at(offset):
                if isinstance(p, int) and p + offset < 0:
                    return below[low[(field, p + offset)]]
                if isinstance(p, int) and p + offset >= layers:
                    return above[high[(field, p + offset - layers)]]
                return moving[field, p + offset]

            return at

        def x(field):
            return lambda offset: wide[field, p, pl.ds(PAD + offset, columns)]

        if kind == "speed":
            b = dtb[p]
            new[0, p] = speed[0, p] + b * (
                diff_forward(x(0)) + backward_y(stress[1, p]) + diff_backward(z(2))
            )
            new[1, p] = speed[1, p] + b * (
                diff_backward(x(1)) + forward_y(stress[5, p]) + diff_backward(z(3))
            )
            vz = speed[2, p] + b * (
                diff_backward(x(2)) + backward_y(stress[3, p]) + diff_forward(z(4))
            )
            new[2, p] = vz
            if isinstance(p, int) and p == 0:
                lift_out[0] = lift_in[...] + time_step * vz
                lift_out[1] = vz
        else:
            l, s = dtl[p], dts[p]
            vx, vy, vz = speed[0, p], speed[1, p], speed[2, p]
            ex, ey, ez = diff_backward(x(0)), backward_y(vy), diff_backward(z(2))
            spread = l * (ex + ey + ez)
            s2 = 2.0 * s
            new[0, p] = stress[0, p] + (spread + s2 * ex)
            new[4, p] = stress[4, p] + (spread + s2 * ez)
            new[5, p] = stress[5, p] + (spread + s2 * ey)
            new[1, p] = stress[1, p] + s * (forward_y(vx) + diff_forward(x(1)))
            new[2, p] = stress[2, p] + s * (diff_forward(z(0)) + diff_forward(x(2)))
            new[3, p] = stress[3, p] + s * (diff_forward(z(1)) + forward_y(vz))

    for p in (0, 1, layers - 2, layers - 1):
        layer(p)

    def body(p, _):
        layer(p)
        return 0

    lax.fori_loop(2, layers - 2, body, 0)
    if not last:

        def read(field, at_layer, at_column):
            if at_column is None:
                return new[field, at_layer]
            return new[field, :, at_column]

        emit_all(out_map, out_depth, read, layers, columns, outs[:n_depth], outs[n_depth : n_depth + 2])
        if kind == "speed":

            @pl.when(even("depth"))
            def _():
                outs[0][pl.ds(SLOTS, 2)] = lift_out[...]


def params(**kw):
    return pltpu.CompilerParams(vmem_limit_bytes=24 << 20, **kw)


def run_half(kind, args, recv_depth, recv_map, last=False):
    layers, columns = args[0].shape[1:3]
    n_depth = len(recv_depth)
    plane = (columns, LANES)
    out = [jax.ShapeDtypeStruct(args[0].shape, F32)]
    if kind == "speed":
        out.append(jax.ShapeDtypeStruct((2,) + plane, F32))
    if not last:
        extra = 2 if kind == "speed" else 0
        out += [jax.ShapeDtypeStruct((SLOTS + extra,) + plane, F32)] * n_depth
        out += [jax.ShapeDtypeStruct((SLOTS, layers, LANES), F32)] * 2

    def kernel(*refs):
        half_step(kind, n_depth, last, refs)

    ins = list(args) + list(recv_depth) + list(recv_map)
    return pl.pallas_call(
        kernel,
        out_shape=out,
        in_specs=[VMEM] * len(ins),
        out_specs=[VMEM] * len(out),
        scratch_shapes=[
            pltpu.VMEM((SLOTS,) + plane, F32),
            pltpu.VMEM((SLOTS,) + plane, F32),
            pltpu.VMEM((3, layers, columns + 2 * PAD, LANES), F32),
        ],
        compiler_params=params(),
        name=kind,
    )(*ins)


def exchange(sends, n_depth):
    depth = [swap(sends[i], "depth", i) for i in range(n_depth)]
    return depth, [swap(sends[n_depth + i], "map", i) for i in range(2)]


OCEAN = ("height", "wet", "index", "flux_x", "flux_y", "depth_x", "depth_y")


def ocean_prep_kernel(n_depth, *refs):
    n = len(OCEAN)
    own, recv = refs[:n], refs[n : n + n_depth]
    wides = refs[n + n_depth : 2 * n + n_depth]
    to_west, to_east = refs[2 * n + n_depth :]
    rows, cols = own[0].shape
    tiles = cols // LANES
    lane = lax.broadcasted_iota(jnp.int32, (rows + 2 * PAD, LANES), 1)
    west = jnp.zeros((rows + 2 * PAD, LANES), F32)
    east = west

    def lines(ref, i, k, t):
        return ref[SLOTS, pl.ds((i * 2 + k) * tiles + t, 1), :]

    for i in range(n):
        wide = wides[i]
        wide[pl.ds(0, PAD)] = jnp.zeros((PAD, cols), F32)
        wide[pl.ds(PAD + rows, PAD)] = jnp.zeros((PAD, cols), F32)
        wide[pl.ds(PAD, rows)] = own[i][...].astype(F32)

        def put(ref, side):
            for k in range(2):
                at = PAD - 2 + k if side == 0 else PAD + rows + k
                for t in range(tiles):
                    wide[pl.ds(at, 1), pl.ds(t * LANES, LANES)] = lines(ref, i, k, t)

        @pl.when(even("depth"))
        def _():
            put(recv[0], 1)
            if n_depth > 1:
                put(recv[1], 0)

        @pl.when(jnp.logical_not(even("depth")))
        def _():
            put(recv[0], 0)
            if n_depth > 1:
                put(recv[1], 1)

        here = jnp.logical_or(lane == 2 * i, lane == 2 * i + 1)
        west = jnp.where(here, roll(wide[:, pl.ds(0, LANES)], 2 * i), west)
        east = jnp.where(here, roll(wide[:, pl.ds(cols - LANES, LANES)], 2 * i + 2), east)
    to_west[...] = west
    to_east[...] = east


def ocean_pick_kernel(own_table, far_table, index, height, wet, west, east, level, source, first, second):
    rows, cols = index.shape
    crust = own_table.shape[1]
    tiles = cols // LANES

    def pick(table):
        def body(i, _):
            at = pl.multiple_of(i * 8, 8)
            for t in range(tiles):
                here = (pl.ds(at, 8), pl.ds(t * LANES, LANES))
                cell = index[here].astype(jnp.int32)
                upper, lower = cell // LANES, lax.rem(cell, LANES)
                a = jnp.zeros((8, LANES), F32)
                b = jnp.zeros((8, LANES), F32)
                for row in range(crust):
                    chosen = upper == row
                    la = jnp.broadcast_to(table(0, row), (8, LANES))
                    lb = jnp.broadcast_to(table(1, row), (8, LANES))
                    a = jnp.where(chosen, jnp.take_along_axis(la, lower, axis=1), a)
                    b = jnp.where(chosen, jnp.take_along_axis(lb, lower, axis=1), b)
                w = wet[here]
                level[here] = w * (height[here] + a)
                source[here] = w * b
            return 0

        lax.fori_loop(0, rows // 8, body, 0)

    @pl.when(lax.axis_index("depth") == 0)
    def _():
        pick(lambda k, row: own_table[k, pl.ds(row, 1)])

    @pl.when(lax.axis_index("depth") != 0)
    def _():
        pick(lambda k, row: far_table[far_table.shape[0] - 2 + k, pl.ds(row, 1)])

    lane = lax.broadcasted_iota(jnp.int32, (rows, LANES), 1)

    def packed(static, start, shift):
        out = static[...]
        for i, ref in ((0, level), (2, source)):
            here = jnp.logical_or(lane == 2 * i, lane == 2 * i + 1)
            out = jnp.where(here, roll(ref[:, pl.ds(start, LANES)], 2 * i + shift), out)
        return out

    to_west = packed(west, 0, 0)
    to_east = packed(east, cols - LANES, 2)

    @pl.when(even("map"))
    def _():
        first[...] = to_east
        second[...] = to_west

    @pl.when(jnp.logical_not(even("map")))
    def _():
        first[...] = to_west
        second[...] = to_east


def ocean_kernel(*refs):
    n = len(OCEAN)
    wides, (first, second) = refs[:n], refs[n : n + 2]
    height_out, flux_out = refs[n + 2 : n + 4]
    full = refs[n + 4]
    height, cols = wides[0].shape
    rows = height - 2 * PAD
    lane = lax.broadcasted_iota(jnp.int32, (height, LANES), 1)

    def fill(east, west):
        e, w = east[...], west[...]
        for i in range(n):
            full[i, :, pl.ds(0, cols)] = wides[i][...]
            beside = jnp.where(lane < 2, roll(e, -2 * i), 0.0)
            full[i, :, pl.ds(cols, LANES)] = jnp.where(lane >= LANES - 2, roll(w, -2 - 2 * i), beside)

    @pl.when(even("map"))
    def _():
        fill(first, second)

    @pl.when(jnp.logical_not(even("map")))
    def _():
        fill(second, first)

    def row_roll(x, by):
        return pltpu.roll(x, by % height, 0)

    level, wet, source, flux_x, flux_y, depth_x, depth_y = (full[i] for i in range(n))
    mask_x = wet * roll(wet, -1)
    mask_y = wet * row_roll(wet, -1)
    depth_x, depth_y = depth_x * mask_x, depth_y * mask_y
    flux_x, flux_y = flux_x * mask_x, flux_y * mask_y
    for _ in range(OSTEPS):
        flux_x = flux_x - ocean_step * gravity * depth_x * (roll(level, -1) - level)
        flux_y = flux_y - ocean_step * gravity * depth_y * (row_roll(level, -1) - level)
        level = (
            level
            - ocean_step * wet * ((flux_x - roll(flux_x, 1)) + (flux_y - row_roll(flux_y, 1)))
            + ocean_step * source
        )
    own = slice(PAD, PAD + rows)
    height_out[...] = level[own, :cols]
    flux_out[0] = flux_x[own, :cols]
    flux_out[1] = flux_y[own, :cols]


def call(kernel, out, ins, name, in_specs=None, scratch=()):
    return pl.pallas_call(
        kernel,
        out_shape=out,
        in_specs=in_specs or [VMEM] * len(ins),
        out_specs=[VMEM] * len(out),
        scratch_shapes=list(scratch),
        compiler_params=params(),
        name=name,
    )(*ins)


def per_device(
    velocity,
    stress,
    region,
    lame_table,
    shear_table,
    buoyancy_table,
    height,
    discharge,
    face_depth,
    wet,
    seafloor_index,
):
    layers, columns = region.shape[:2]
    rows, cols = height.shape
    n_depth = min(2, lax.axis_size("depth") - 1)
    shape = jax.ShapeDtypeStruct
    plane = (columns, LANES)
    ocean = [
        height,
        wet.astype(F32),
        seafloor_index.astype(F32),
        discharge[0],
        discharge[1],
        face_depth[0],
        face_depth[1],
    ]
    n = len(ocean)
    sends = call(
        functools.partial(edge_kernel, n_depth, n, layers, columns),
        [shape((SLOTS + 1,) + plane, F32)] * n_depth + [shape((SLOTS, layers, LANES), F32)] * 2,
        [stress] + ocean,
        "edges",
        in_specs=[ANY] * (1 + n),
        scratch=[
            pltpu.VMEM((3, layers, PAD, LANES), F32),
            pltpu.VMEM((3, layers, PAD, LANES), F32),
            pltpu.VMEM((3, 2) + plane, F32),
            pltpu.VMEM((3, 2) + plane, F32),
            pltpu.VMEM((n, PAD, cols), F32),
            pltpu.VMEM((n, PAD, cols), F32),
            pltpu.SemaphoreType.DMA((4 + 2 * n,)),
        ],
    )
    recv = exchange(sends, n_depth)
    dtb, dtl, dts = call(
        material_kernel,
        [shape(region.shape, F32)] * 3,
        [lame_table, shear_table, buoyancy_table, region],
        "material",
        in_specs=[SMEM] * 3 + [VMEM],
    )
    tall = (rows + 2 * PAD, cols)
    *wides, west, east = call(
        functools.partial(ocean_prep_kernel, n_depth),
        [shape(tall, F32)] * n + [shape((tall[0], LANES), F32)] * 2,
        ocean + recv[0],
        "ocean_prep",
    )
    speeds, forces, lift = velocity, stress, jnp.zeros(plane, F32)
    for turn in range(ITERS):
        speeds, table, *sends = run_half("speed", (speeds, forces, dtb, lift), *recv)
        lift = table[0]
        recv = exchange(sends, n_depth)
        last = turn == ITERS - 1
        forces, *sends = run_half("stress", (forces, speeds, dtl, dts), *recv, last=last)
        if not last:
            recv = exchange(sends, n_depth)
    if n_depth > 1:
        mine = lax.axis_index("depth") == 0
        table = lax.psum(jnp.where(mine, table, jnp.zeros_like(table)), "depth")
        far = table
    else:
        far = recv[0][0]
    level, source, first, second = call(
        ocean_pick_kernel,
        [shape(tall, F32)] * 2 + [shape((tall[0], LANES), F32)] * 2,
        [table, far, wides[2], wides[0], wides[1], west, east],
        "ocean_pick",
    )
    first, second = swap(first, "map", 0), swap(second, "map", 1)
    level_out, flux_out = call(
        ocean_kernel,
        [shape((rows, cols), F32), shape((2, rows, cols), F32)],
        [level, wides[1], source] + list(wides[3:]) + [first, second],
        "ocean",
        scratch=[pltpu.VMEM((n, tall[0], cols + LANES), F32)],
    )
    return (speeds, forces, level_out, flux_out)


def solution(mesh):
    return jax.shard_map(
        per_device,
        mesh=mesh,
        in_specs=(
            P(None, "depth", "map", None),
            P(None, "depth", "map", None),
            P("depth", "map", None),
            P(),
            P(),
            P(),
            P("depth", "map"),
            P(None, "depth", "map"),
            P(None, "depth", "map"),
            P("depth", "map"),
            P("depth", "map"),
        ),
        out_specs=(
            P(None, "depth", "map", None),
            P(None, "depth", "map", None),
            P("depth", "map"),
            P(None, "depth", "map"),
        ),
        check_vma=False,
    )
```

time: 254 us -> 76.6 us (0.30)
  other arithmetic: 72.3 us -> 1.95 us
  starting transfers between devices: 91.2 us -> 31.8 us
  local copies, waits for them, and re-layouts: 39.5 us -> 2.15 us
  Pallas kernels: 0 us -> 20.6 us
  matrix products: 16.4 us -> 0 us
  blocking collectives: 7.31 us -> 0 us
  waiting for transfers between devices: 21.9 us -> 18 us
    ppermute x32 -> x20, starting transfers between devices: 91.2 us -> 31.8 us  [swap(): return lax.ppermute(x, axis, swap_pairs(lax.axis_size(axis))[phase])]
    slice x73 -> x0, local copies, waits for them, and re-layouts: 31.2 us -> none  [the longest x18 8.92 us: forward_y(): jnp.roll(field, 1, 2)]
    add x19 -> x0, other arithmetic: 28.4 us -> none  [the longest x2 11.2 us: per_device(): forces[5] + time_step * (lame * spread + 2.0 * shear * strain_y)]
    select_n x32 -> x0, other arithmetic: 22.6 us -> none  [the longest x16 11.3 us: one_block(): lower = indices % tile_cols]
    pallas_call x0 -> x11, Pallas kernels: none -> 20.6 us  [the longest x6 12.7 us: run_half(): pl.pallas_call(kernel, out_shape=out, in_specs=[VMEM] * len(ins), out_spe...]
    dot_general x16 -> x0, matrix products: 16.4 us -> none  [one_block(): jnp.einsum('rck,kn->rcn', onehot, table, precision=lax.Precision.HIGHEST)]
    dynamic_update_slice x16 -> x0, other arithmetic: 9.69 us -> none  [seafloor_pick(): result = lax.map(one_block, blocks)]
    psum x1 -> x0, blocking collectives: 7.31 us -> none  [broadcast(): return lax.psum(jnp.where(mine, x, jnp.zeros_like(x)), axis)]
  transfers between devices with their start and end apart: 32 -> 20, of which waited for: 11 -> 7; matrix products, arithmetic and copies ran while one was open for 10% -> 0% of each run, Pallas kernels for 0% -> 6%
where the time goes in v1:
time: 76.6 us; the launch traced here: 75.3 us
  starting transfers between devices  31.8 us (42%)
  Pallas kernels  20.6 us (27%)
  waiting for transfers between devices  18 us (23%)
  local copies, waits for them, and re-layouts  2.15 us (3%)
  other arithmetic  1.95 us (3%)
  between operations  0.93 us (1%)
    ppermute x20, starting transfers between devices, swap(): return lax.ppermute(x, axis, swap_pairs(lax.axis_size(axis))[phase])  31.8 us
    ppermute x20, waiting for transfers between devices, swap(): return lax.ppermute(x, axis, swap_pairs(lax.axis_size(axis))[phase])  18 us
    pallas_call x6, Pallas kernels, run_half(): pl.pallas_call(kernel, out_shape=out, in_specs=[VMEM] * len(ins), out_spe...  12.7 us
    pallas_call x5, Pallas kernels, call(): pl.pallas_call(kernel, out_shape=out, in_specs=in_specs or [VMEM] * len(i...  7.86 us
  transfers between devices with their start and end apart: 20, of which 7 were waited for; matrix products, arithmetic and copies ran while one was open for 0% of the time, Pallas kernels for 6%

profile of v1, /device:TPU:7, one launch (start us, length us, event | category | flops | bytes accessed | tf_op | source)
XLA Modules:
  0.0 75.3 jit_solution(14643006148754261898)
XLA Ops:
  6.6 3.0 %collective-permute-start.2 = (f32[5,16,128]{2,1,0:T(8,128)S(1)}, f32[5,16,128]{2,1,0:T(8,128)S(1)}, u32[]{:S(2)}, u32[]{:S(2)}) collective-permute-start(f32[5,16,128]{2,1,0:T(8,128)S(1)} %get-tuple-element.51), channel_id=1, source_target_pairs={{1,2},{2,1},{3,4},{4,3},{5,6},{6,5},{7,8},{8,7},{9,10},{10,9},{11,... | collective-permute-start | bytes 122888 | tf_op jit(solution)/shard_map/ppermute | solution.py:51
  10.7 2.2 %collective-permute-done.2.refs_6_ = f32[5,16,128]{2,1,0:T(8,128)S(1)} collective-permute-done((f32[5,16,128]{2,1,0:T(8,128)S(1)}, f32[5,16,128]{2,1,0:T(8,128)S(1)}, u32[]{:S(2)}, u32[]{:S(2)}) %collective-permute-start.2) | collective-permute-done | bytes 40992 | tf_op jit(solution)/shard_map/ppermute | solution.py:51
  12.8 1.8 %speed.3 = (f32[3,16,32,128]{3,2,1,0:T(8,128)S(1)}, f32[2,32,128]{2,1,0:T(8,128)S(1)}, f32[7,32,128]{2,1,0:T(8,128)S(1)}, f32[5,16,128]{2,1,0:T(8,128)S(1)}, f32[5,16,128]{2,1,0:T(8,128)S(1)}) custom-call(f32[3,16,32,128]{3,2,1,0:T(8,128)S(1)} %copy-done.2, f32[6,16,32,128]{3,2,1,0:T(8,128)S(1)} %copy-done, f32[16,32,128]{2,1,0:T(8,128)S(1)} %get-tuple-element.48.refs_2_, ...), custom_call_target="tpu_custom_call" | custom-call | tf_op jit(solution)/shard_map/speed/pallas_call | solution.py:324
  14.7 1.3 %collective-permute-start.3 = (f32[7,32,128]{2,1,0:T(8,128)S(1)}, f32[7,32,128]{2,1,0:T(8,128)S(1)}, u32[]{:S(2)}, u32[]{:S(2)}) collective-permute-start(f32[7,32,128]{2,1,0:T(8,128)S(1)} %get-tuple-element.55), channel_id=1, source_target_pairs={{0,16},{16,0},{1,17},{17,1},{2,18},{18,2},{3,19},{19,3},{4,20},{20... | collective-permute-start | bytes 344072 | tf_op jit(solution)/shard_map/ppermute | solution.py:51
  15.9 3.4 %collective-permute-start.5 = (f32[5,16,128]{2,1,0:T(8,128)S(1)}, f32[5,16,128]{2,1,0:T(8,128)S(1)}, u32[]{:S(2)}, u32[]{:S(2)}) collective-permute-start(f32[5,16,128]{2,1,0:T(8,128)S(1)} %get-tuple-element.57), channel_id=1, source_target_pairs={{1,2},{2,1},{3,4},{4,3},{5,6},{6,5},{7,8},{8,7},{9,10},{10,9},{11,... | collective-permute-start | bytes 122888 | tf_op jit(solution)/shard_map/ppermute | solution.py:51
  19.4 2.8 %collective-permute-done.5.refs_6_ = f32[5,16,128]{2,1,0:T(8,128)S(1)} collective-permute-done((f32[5,16,128]{2,1,0:T(8,128)S(1)}, f32[5,16,128]{2,1,0:T(8,128)S(1)}, u32[]{:S(2)}, u32[]{:S(2)}) %collective-permute-start.5) | collective-permute-done | bytes 40992 | tf_op jit(solution)/shard_map/ppermute | solution.py:51
  22.2 1.8 %stress.5 = (f32[6,16,32,128]{3,2,1,0:T(8,128)S(1)}, f32[5,32,128]{2,1,0:T(8,128)S(1)}, f32[5,16,128]{2,1,0:T(8,128)S(1)}, f32[5,16,128]{2,1,0:T(8,128)S(1)}) custom-call(f32[6,16,32,128]{3,2,1,0:T(8,128)S(1)} %copy-done, f32[3,16,32,128]{3,2,1,0:T(8,128)S(1)} %get-tuple-element.52.refs_1_.refs_0_, f32[16,32,128]{2,1,0:T(8,128)S(1)} %get-tuple-element.53.refs_2_, ...), custom_call_target="tpu_custom_call" | custom-call | tf_op jit(solution)/shard_map/stress/pallas_call | solution.py:324
  24.3 3.8 %collective-permute-start.8 = (f32[5,16,128]{2,1,0:T(8,128)S(1)}, f32[5,16,128]{2,1,0:T(8,128)S(1)}, u32[]{:S(2)}, u32[]{:S(2)}) collective-permute-start(f32[5,16,128]{2,1,0:T(8,128)S(1)} %get-tuple-element.62), channel_id=1, source_target_pairs={{1,2},{2,1},{3,4},{4,3},{5,6},{6,5},{7,8},{8,7},{9,10},{10,9},{11,... | collective-permute-start | bytes 122888 | tf_op jit(solution)/shard_map/ppermute | solution.py:51
  28.1 2.4 %collective-permute-done.8.refs_6_ = f32[5,16,128]{2,1,0:T(8,128)S(1)} collective-permute-done((f32[5,16,128]{2,1,0:T(8,128)S(1)}, f32[5,16,128]{2,1,0:T(8,128)S(1)}, u32[]{:S(2)}, u32[]{:S(2)}) %collective-permute-start.8) | collective-permute-done | bytes 40992 | tf_op jit(solution)/shard_map/ppermute | solution.py:51
  30.5 1.8 %speed.4 = (f32[3,16,32,128]{3,2,1,0:T(8,128)S(1)}, f32[2,32,128]{2,1,0:T(8,128)S(1)}, f32[7,32,128]{2,1,0:T(8,128)S(1)}, f32[5,16,128]{2,1,0:T(8,128)S(1)}, f32[5,16,128]{2,1,0:T(8,128)S(1)}) custom-call(f32[3,16,32,128]{3,2,1,0:T(8,128)S(1)} %get-tuple-element.52.refs_1_.refs_0_, f32[6,16,32,128]{3,2,1,0:T(8,128)S(1)} %get-tuple-element.58.refs_1_.refs_0_, ...), custom_call_target="tpu_custom_call" | custom-call | tf_op jit(solution)/shard_map/speed/pallas_call | solution.py:324
  32.3 1.3 %collective-permute-start.9 = (f32[7,32,128]{2,1,0:T(8,128)S(1)}, f32[7,32,128]{2,1,0:T(8,128)S(1)}, u32[]{:S(2)}, u32[]{:S(2)}) collective-permute-start(f32[7,32,128]{2,1,0:T(8,128)S(1)} %get-tuple-element.64), channel_id=1, source_target_pairs={{0,16},{16,0},{1,17},{17,1},{2,18},{18,2},{3,19},{19,3},{4,20},{20... | collective-permute-start | bytes 344072 | tf_op jit(solution)/shard_map/ppermute | solution.py:51
  33.6 4.1 %collective-permute-start.11 = (f32[5,16,128]{2,1,0:T(8,128)S(1)}, f32[5,16,128]{2,1,0:T(8,128)S(1)}, u32[]{:S(2)}, u32[]{:S(2)}) collective-permute-start(f32[5,16,128]{2,1,0:T(8,128)S(1)} %get-tuple-element.66), channel_id=1, source_target_pairs={{1,2},{2,1},{3,4},{4,3},{5,6},{6,5},{7,8},{8,7},{9,10},{10,9},{11,... | collective-permute-start | bytes 122888 | tf_op jit(solution)/shard_map/ppermute | solution.py:51
  37.7 2.0 %collective-permute-done.11.refs_6_ = f32[5,16,128]{2,1,0:T(8,128)S(1)} collective-permute-done((f32[5,16,128]{2,1,0:T(8,128)S(1)}, f32[5,16,128]{2,1,0:T(8,128)S(1)}, u32[]{:S(2)}, u32[]{:S(2)}) %collective-permute-start.11) | collective-permute-done | bytes 40992 | tf_op jit(solution)/shard_map/ppermute | solution.py:51
  39.8 1.8 %stress.6 = (f32[6,16,32,128]{3,2,1,0:T(8,128)S(1)}, f32[5,32,128]{2,1,0:T(8,128)S(1)}, f32[5,16,128]{2,1,0:T(8,128)S(1)}, f32[5,16,128]{2,1,0:T(8,128)S(1)}) custom-call(f32[6,16,32,128]{3,2,1,0:T(8,128)S(1)} %get-tuple-element.58.refs_1_.refs_0_, f32[3,16,32,128]{3,2,1,0:T(8,128)S(1)} %get-tuple-element.63.refs_1_.refs_0_, ...), custom_call_target="tpu_custom_call" | custom-call | tf_op jit(solution)/shard_map/stress/pallas_call | solution.py:324
  41.9 4.5 %collective-permute-start.14 = (f32[5,16,128]{2,1,0:T(8,128)S(1)}, f32[5,16,128]{2,1,0:T(8,128)S(1)}, u32[]{:S(2)}, u32[]{:S(2)}) collective-permute-start(f32[5,16,128]{2,1,0:T(8,128)S(1)} %get-tuple-element.71), channel_id=1, source_target_pairs={{1,2},{2,1},{3,4},{4,3},{5,6},{6,5},{7,8},{8,7},{9,10},{10,9},{11,... | collective-permute-start | bytes 122888 | tf_op jit(solution)/shard_map/ppermute | solution.py:51
  46.4 1.7 %collective-permute-done.14.refs_6_ = f32[5,16,128]{2,1,0:T(8,128)S(1)} collective-permute-done((f32[5,16,128]{2,1,0:T(8,128)S(1)}, f32[5,16,128]{2,1,0:T(8,128)S(1)}, u32[]{:S(2)}, u32[]{:S(2)}) %collective-permute-start.14) | collective-permute-done | bytes 40992 | tf_op jit(solution)/shard_map/ppermute | solution.py:51
  48.1 2.7 %speed.5 = (f32[3,16,32,128]{3,2,1,0:T(8,128)}, f32[2,32,128]{2,1,0:T(8,128)S(1)}, f32[7,32,128]{2,1,0:T(8,128)S(1)}, f32[5,16,128]{2,1,0:T(8,128)S(1)}, f32[5,16,128]{2,1,0:T(8,128)S(1)}) custom-call(f32[3,16,32,128]{3,2,1,0:T(8,128)S(1)} %get-tuple-element.63.refs_1_.refs_0_, f32[6,16,32,128]{3,2,1,0:T(8,128)S(1)} %get-tuple-element.67.refs_1_.refs_0_, ...), custom_call_target="tpu_custom_call" | custom-call | tf_op jit(solution)/shard_map/speed/pallas_call | solution.py:324
  52.8 3.1 %collective-permute-done.15.refs_4_.far_table = f32[7,32,128]{2,1,0:T(8,128)S(1)} collective-permute-done((f32[7,32,128]{2,1,0:T(8,128)S(1)}, f32[7,32,128]{2,1,0:T(8,128)S(1)}, u32[]{:S(2)}, u32[]{:S(2)}) %collective-permute-start.15) | collective-permute-done | bytes 114720 | tf_op jit(solution)/shard_map/ppermute | solution.py:51
  55.9 4.1 %ocean_pick.1 = (f32[144,256]{1,0:T(8,128)S(1)}, f32[144,256]{1,0:T(8,128)S(1)}, f32[144,128]{1,0:T(8,128)S(1)}, f32[144,128]{1,0:T(8,128)S(1)}) custom-call(f32[2,32,128]{2,1,0:T(8,128)S(1)} %get-tuple-element.76.own_table, f32[7,32,128]{2,1,0:T(8,128)S(1)} %collective-permute-done.15.refs_4_.far_table, f32[144,256]{1,0:T(8,128)S(1)} %get-tuple-element.77.index, ...), custom_call_target="tpu_custom_call" | custom-call | tf_op jit(solution)/shard_map/ocean_pick/pallas_call | solution.py:497
  60.5 4.2 %collective-permute-start.19 = (f32[144,128]{1,0:T(8,128)S(1)}, f32[144,128]{1,0:T(8,128)S(1)}, u32[]{:S(2)}, u32[]{:S(2)}) collective-permute-start(f32[144,128]{1,0:T(8,128)S(1)} %get-tuple-element.89), channel_id=1, source_target_pairs={{1,2},{2,1},{3,4},{4,3},{5,6},{6,5},{7,8},{8,7},{9,10},{10,9},{11,... | collective-permute-start | bytes 221192 | tf_op jit(solution)/shard_map/ppermute | solution.py:51
  64.7 2.4 %collective-permute-start.17 = (f32[5,16,128]{2,1,0:T(8,128)S(1)}, f32[5,16,128]{2,1,0:T(8,128)S(1)}, u32[]{:S(2)}, u32[]{:S(2)}) collective-permute-start(f32[5,16,128]{2,1,0:T(8,128)S(1)} %get-tuple-element.75), channel_id=1, source_target_pairs={{1,2},{2,1},{3,4},{4,3},{5,6},{6,5},{7,8},{8,7},{9,10},{10,9},{11,... | collective-permute-start | bytes 122888 | tf_op jit(solution)/shard_map/ppermute | solution.py:51
  67.2 3.8 %collective-permute-done.17.refs_6_ = f32[5,16,128]{2,1,0:T(8,128)S(1)} collective-permute-done((f32[5,16,128]{2,1,0:T(8,128)S(1)}, f32[5,16,128]{2,1,0:T(8,128)S(1)}, u32[]{:S(2)}, u32[]{:S(2)}) %collective-permute-start.17) | collective-permute-done | bytes 40992 | tf_op jit(solution)/shard_map/ppermute | solution.py:51
  71.0 2.9 %stress.7 = f32[6,16,32,128]{3,2,1,0:T(8,128)} custom-call(f32[6,16,32,128]{3,2,1,0:T(8,128)S(1)} %get-tuple-element.67.refs_1_.refs_0_, f32[3,16,32,128]{3,2,1,0:T(8,128)S(1)} %copy-done.1, f32[16,32,128]{2,1,0:T(8,128)S(1)} %get-tuple-element.53.refs_2_, f32[16,32,128]{2,1,0:T(8,128)S(1)} %get-tuple-element.54.refs_3_, ...), custom_call_target="tpu_custom_call" | custom-call | tf_op jit(solution)/shard_map/stress/pallas_call | solution.py:324
  73.8 1.5 %ocean.1 = (f32[128,256]{1,0:T(8,128)}, f32[2,128,256]{2,1,0:T(8,128)}) custom-call(f32[144,256]{1,0:T(8,128)S(1)} %get-tuple-element.82.refs_0_, f32[144,256]{1,0:T(8,128)S(1)} %get-tuple-element.79.wet.refs_1_, f32[144,256]{1,0:T(8,128)S(1)} %get-tuple-element.83.refs_2_, f32[144,256]{1,0:T(8,128)S(1)} %get-tuple-element.84.refs_3_, ...), custom_call_target="tpu_custom_call" | custom-call | tf_op jit(solution)/shard_map/ocean/pallas_call | solution.py:497
  (51 shorter events, 10.2 us)
Async XLA Ops:
  3.7 9.1 %copy-start.2 = (f32[3,16,32,128]{3,2,1,0:T(8,128)S(1)}, f32[3,16,32,128]{3,2,1,0:T(8,128)}, u32[]{:S(2)}) copy-start(f32[3,16,32,128]{3,2,1,0:T(8,128)} %refs_0_.5) | copy-start | bytes 2359300
  4.7 4.9 %copy-start.8 = (f32[8]{0:T(128)S(1)}, f32[8]{0:T(128)}, u32[]{:S(2)}) copy-start(f32[8]{0:T(128)} %buoy_t.1) | copy-start | bytes 100
  5.3 7.5 %collective-permute-start = (f32[6,32,128]{2,1,0:T(8,128)S(1)}, f32[6,32,128]{2,1,0:T(8,128)S(1)}, u32[]{:S(2)}, u32[]{:S(2)}) collective-permute-start(f32[6,32,128]{2,1,0:T(8,128)S(1)} %get-tuple-element.49), channel_id=1, source_target_pairs={{0,16},{16,0},{1,17},{17,1},{2,18},{18,2},{3,19},{19,3},{4,20},{20... | collective-permute-start | bytes 294920 | tf_op jit(solution)/shard_map/ppermute | solution.py:51
  5.6 5.0 %collective-permute-start.1 = (f32[5,16,128]{2,1,0:T(8,128)S(1)}, f32[5,16,128]{2,1,0:T(8,128)S(1)}, u32[]{:S(2)}, u32[]{:S(2)}) collective-permute-start(f32[5,16,128]{2,1,0:T(8,128)S(1)} %get-tuple-element.50), channel_id=1, source_target_pairs={{0,1},{1,0},{2,3},{3,2},{4,5},{5,4},{6,7},{7,6},{8,9},{9,8},{10,11... | collective-permute-start | bytes 122888 | tf_op jit(solution)/shard_map/ppermute | solution.py:51
  6.6 6.2 %collective-permute-start.2 = (f32[5,16,128]{2,1,0:T(8,128)S(1)}, f32[5,16,128]{2,1,0:T(8,128)S(1)}, u32[]{:S(2)}, u32[]{:S(2)}) collective-permute-start(f32[5,16,128]{2,1,0:T(8,128)S(1)} %get-tuple-element.51), channel_id=1, source_target_pairs={{1,2},{2,1},{3,4},{4,3},{5,6},{6,5},{7,8},{8,7},{9,10},{10,9},{11,... | collective-permute-start | bytes 122888 | tf_op jit(solution)/shard_map/ppermute | solution.py:51
  14.7 7.5 %collective-permute-start.3 = (f32[7,32,128]{2,1,0:T(8,128)S(1)}, f32[7,32,128]{2,1,0:T(8,128)S(1)}, u32[]{:S(2)}, u32[]{:S(2)}) collective-permute-start(f32[7,32,128]{2,1,0:T(8,128)S(1)} %get-tuple-element.55), channel_id=1, source_target_pairs={{0,16},{16,0},{1,17},{17,1},{2,18},{18,2},{3,19},{19,3},{4,20},{20... | collective-permute-start | bytes 344072 | tf_op jit(solution)/shard_map/ppermute | solution.py:51
  15.9 3.4 %collective-permute-start.4 = (f32[5,16,128]{2,1,0:T(8,128)S(1)}, f32[5,16,128]{2,1,0:T(8,128)S(1)}, u32[]{:S(2)}, u32[]{:S(2)}) collective-permute-start(f32[5,16,128]{2,1,0:T(8,128)S(1)} %get-tuple-element.56), channel_id=1, source_target_pairs={{0,1},{1,0},{2,3},{3,2},{4,5},{5,4},{6,7},{7,6},{8,9},{9,8},{10,11... | collective-permute-start | bytes 122888 | tf_op jit(solution)/shard_map/ppermute | solution.py:51
  15.9 6.2 %collective-permute-start.5 = (f32[5,16,128]{2,1,0:T(8,128)S(1)}, f32[5,16,128]{2,1,0:T(8,128)S(1)}, u32[]{:S(2)}, u32[]{:S(2)}) collective-permute-start(f32[5,16,128]{2,1,0:T(8,128)S(1)} %get-tuple-element.57), channel_id=1, source_target_pairs={{1,2},{2,1},{3,4},{4,3},{5,6},{6,5},{7,8},{8,7},{9,10},{10,9},{11,... | collective-permute-start | bytes 122888 | tf_op jit(solution)/shard_map/ppermute | solution.py:51
  23.9 6.5 %collective-permute-start.6 = (f32[5,32,128]{2,1,0:T(8,128)S(1)}, f32[5,32,128]{2,1,0:T(8,128)S(1)}, u32[]{:S(2)}, u32[]{:S(2)}) collective-permute-start(f32[5,32,128]{2,1,0:T(8,128)S(1)} %get-tuple-element.60), channel_id=1, source_target_pairs={{0,16},{16,0},{1,17},{17,1},{2,18},{18,2},{3,19},{19,3},{4,20},{20... | collective-permute-start | bytes 245768 | tf_op jit(solution)/shard_map/ppermute | solution.py:51
  24.2 3.8 %collective-permute-start.7 = (f32[5,16,128]{2,1,0:T(8,128)S(1)}, f32[5,16,128]{2,1,0:T(8,128)S(1)}, u32[]{:S(2)}, u32[]{:S(2)}) collective-permute-start(f32[5,16,128]{2,1,0:T(8,128)S(1)} %get-tuple-element.61), channel_id=1, source_target_pairs={{0,1},{1,0},{2,3},{3,2},{4,5},{5,4},{6,7},{7,6},{8,9},{9,8},{10,11... | collective-permute-start | bytes 122888 | tf_op jit(solution)/shard_map/ppermute | solution.py:51
  24.3 6.2 %collective-permute-start.8 = (f32[5,16,128]{2,1,0:T(8,128)S(1)}, f32[5,16,128]{2,1,0:T(8,128)S(1)}, u32[]{:S(2)}, u32[]{:S(2)}) collective-permute-start(f32[5,16,128]{2,1,0:T(8,128)S(1)} %get-tuple-element.62), channel_id=1, source_target_pairs={{1,2},{2,1},{3,4},{4,3},{5,6},{6,5},{7,8},{8,7},{9,10},{10,9},{11,... | collective-permute-start | bytes 122888 | tf_op jit(solution)/shard_map/ppermute | solution.py:51
  32.3 7.5 %collective-permute-start.9 = (f32[7,32,128]{2,1,0:T(8,128)S(1)}, f32[7,32,128]{2,1,0:T(8,128)S(1)}, u32[]{:S(2)}, u32[]{:S(2)}) collective-permute-start(f32[7,32,128]{2,1,0:T(8,128)S(1)} %get-tuple-element.64), channel_id=1, source_target_pairs={{0,16},{16,0},{1,17},{17,1},{2,18},{18,2},{3,19},{19,3},{4,20},{20... | collective-permute-start | bytes 344072 | tf_op jit(solution)/shard_map/ppermute | solution.py:51
  33.6 4.2 %collective-permute-start.10 = (f32[5,16,128]{2,1,0:T(8,128)S(1)}, f32[5,16,128]{2,1,0:T(8,128)S(1)}, u32[]{:S(2)}, u32[]{:S(2)}) collective-permute-start(f32[5,16,128]{2,1,0:T(8,128)S(1)} %get-tuple-element.65), channel_id=1, source_target_pairs={{0,1},{1,0},{2,3},{3,2},{4,5},{5,4},{6,7},{7,6},{8,9},{9,8},{10,11... | collective-permute-start | bytes 122888 | tf_op jit(solution)/shard_map/ppermute | solution.py:51
  33.6 6.2 %collective-permute-start.11 = (f32[5,16,128]{2,1,0:T(8,128)S(1)}, f32[5,16,128]{2,1,0:T(8,128)S(1)}, u32[]{:S(2)}, u32[]{:S(2)}) collective-permute-start(f32[5,16,128]{2,1,0:T(8,128)S(1)} %get-tuple-element.66), channel_id=1, source_target_pairs={{1,2},{2,1},{3,4},{4,3},{5,6},{6,5},{7,8},{8,7},{9,10},{10,9},{11,... | collective-permute-start | bytes 122888 | tf_op jit(solution)/shard_map/ppermute | solution.py:51
  41.5 10.5 %copy-start.4 = (f32[128,256]{1,0:T(8,128)S(1)}, f32[128,256]{1,0:T(8,128)}, u32[]{:S(2)}) copy-start(f32[128,256]{1,0:T(8,128)} %refs_0_.7) | copy-start | bytes 393220
  41.6 6.5 %collective-permute-start.12 = (f32[5,32,128]{2,1,0:T(8,128)S(1)}, f32[5,32,128]{2,1,0:T(8,128)S(1)}, u32[]{:S(2)}, u32[]{:S(2)}) collective-permute-start(f32[5,32,128]{2,1,0:T(8,128)S(1)} %get-tuple-element.69), channel_id=1, source_target_pairs={{0,16},{16,0},{1,17},{17,1},{2,18},{18,2},{3,19},{19,3},{4,20},{20... | collective-permute-start | bytes 245768 | tf_op jit(solution)/shard_map/ppermute | solution.py:51
  41.9 4.5 %collective-permute-start.13 = (f32[5,16,128]{2,1,0:T(8,128)S(1)}, f32[5,16,128]{2,1,0:T(8,128)S(1)}, u32[]{:S(2)}, u32[]{:S(2)}) collective-permute-start(f32[5,16,128]{2,1,0:T(8,128)S(1)} %get-tuple-element.70), channel_id=1, source_target_pairs={{0,1},{1,0},{2,3},{3,2},{4,5},{5,4},{6,7},{7,6},{8,9},{9,8},{10,11... | collective-permute-start | bytes 122888 | tf_op jit(solution)/shard_map/ppermute | solution.py:51
  41.9 6.2 %collective-permute-start.14 = (f32[5,16,128]{2,1,0:T(8,128)S(1)}, f32[5,16,128]{2,1,0:T(8,128)S(1)}, u32[]{:S(2)}, u32[]{:S(2)}) collective-permute-start(f32[5,16,128]{2,1,0:T(8,128)S(1)} %get-tuple-element.71), channel_id=1, source_target_pairs={{1,2},{2,1},{3,4},{4,3},{5,6},{6,5},{7,8},{8,7},{9,10},{10,9},{11,... | collective-permute-start | bytes 122888 | tf_op jit(solution)/shard_map/ppermute | solution.py:51
  50.8 20.2 %copy-start.1 = (f32[3,16,32,128]{3,2,1,0:T(8,128)S(1)}, f32[3,16,32,128]{3,2,1,0:T(8,128)}, u32[]{:S(2)}) copy-start(f32[3,16,32,128]{3,2,1,0:T(8,128)} %get-tuple-element.44.refs_1_) | copy-start | bytes 2359300
  50.8 5.1 %collective-permute-start.15 = (f32[7,32,128]{2,1,0:T(8,128)S(1)}, f32[7,32,128]{2,1,0:T(8,128)S(1)}, u32[]{:S(2)}, u32[]{:S(2)}) collective-permute-start(f32[7,32,128]{2,1,0:T(8,128)S(1)} %get-tuple-element.73), channel_id=1, source_target_pairs={{0,16},{16,0},{1,17},{17,1},{2,18},{18,2},{3,19},{19,3},{4,20},{20... | collective-permute-start | bytes 344072 | tf_op jit(solution)/shard_map/ppermute | solution.py:51
  60.0 13.8 %collective-permute-start.18 = (f32[144,128]{1,0:T(8,128)S(1)}, f32[144,128]{1,0:T(8,128)S(1)}, u32[]{:S(2)}, u32[]{:S(2)}) collective-permute-start(f32[144,128]{1,0:T(8,128)S(1)} %get-tuple-element.88), channel_id=1, source_target_pairs={{0,1},{1,0},{2,3},{3,2},{4,5},{5,4},{6,7},{7,6},{8,9},{9,8},{10,11... | collective-permute-start | bytes 221192 | tf_op jit(solution)/shard_map/ppermute | solution.py:51
  60.5 13.3 %collective-permute-start.19 = (f32[144,128]{1,0:T(8,128)S(1)}, f32[144,128]{1,0:T(8,128)S(1)}, u32[]{:S(2)}, u32[]{:S(2)}) collective-permute-start(f32[144,128]{1,0:T(8,128)S(1)} %get-tuple-element.89), channel_id=1, source_target_pairs={{1,2},{2,1},{3,4},{4,3},{5,6},{6,5},{7,8},{8,7},{9,10},{10,9},{11,... | collective-permute-start | bytes 221192 | tf_op jit(solution)/shard_map/ppermute | solution.py:51
  64.6 2.5 %collective-permute-start.16 = (f32[5,16,128]{2,1,0:T(8,128)S(1)}, f32[5,16,128]{2,1,0:T(8,128)S(1)}, u32[]{:S(2)}, u32[]{:S(2)}) collective-permute-start(f32[5,16,128]{2,1,0:T(8,128)S(1)} %get-tuple-element.74), channel_id=1, source_target_pairs={{0,1},{1,0},{2,3},{3,2},{4,5},{5,4},{6,7},{7,6},{8,9},{9,8},{10,11... | collective-permute-start | bytes 122888 | tf_op jit(solution)/shard_map/ppermute | solution.py:51
  64.7 6.2 %collective-permute-start.17 = (f32[5,16,128]{2,1,0:T(8,128)S(1)}, f32[5,16,128]{2,1,0:T(8,128)S(1)}, u32[]{:S(2)}, u32[]{:S(2)}) collective-permute-start(f32[5,16,128]{2,1,0:T(8,128)S(1)} %get-tuple-element.75), channel_id=1, source_target_pairs={{1,2},{2,1},{3,4},{4,3},{5,6},{6,5},{7,8},{8,7},{9,10},{10,9},{11,... | collective-permute-start | bytes 122888 | tf_op jit(solution)/shard_map/ppermute | solution.py:51
  (5 other events, 18.8 us)
